TPU v7x, 32 devices: a whole 2x2x4 slice. The times are simulated.
32 devices in a mesh: tile: 8 (over y, x, core), grp: 4 (over z).
Axes of the slice: x: 2, y: 2, z: 4, core: 2. Of those that a mesh axis runs over, the one named last changes fastest.
Arguments:
- earlier_flow_speeds: float32 [2, 64, 256, 512], P(None, None, 'tile', 'grp'), may hold values from -6 to 6
- flow_rate_factor: float32 [64, 256, 512], P(None, 'tile', 'grp'), may hold values from 0.5 to 2
- scaled_warmth: float32 [64, 256, 512], P('grp', 'tile'), may hold values from -3 to 3
- gravity_forcing: float32 [2, 256, 512], P(None, 'tile', 'grp'), may hold values from -6 to 6
- sliding_coefficient: float32 [256, 512], P('tile', 'grp'), may hold values from 1 to 10
- icy_column_flag: int32 [256, 512], P('tile', 'grp'), may hold values 0 or 1
- resting_on_bed_flag: int32 [256, 512], P('tile', 'grp'), may hold values 0 or 1
Outputs:
- velocity: float32 [2, 64, 256, 512], P(None, None, 'tile', 'grp')
- temperature_next: float32 [64, 256, 512], P('grp', 'tile')
- hardness_next: float32 [64, 256, 512], P(None, 'tile', 'grp')
All inputs are finite; a program needn't handle non-finite values. No bound on the sum of `icy_column_flag` or of `resting_on_bed_flag` on one device may be relied on, other than what follows from the above.
Results may differ from a plain program's by a relative error of at most 0.00002.
Values sent between devices are 32-bit elements; how exact they have to be, the bound alone decides.
A program may use at most 64 MiB of HBM per device.

v0:
```python
import functools

import jax
import jax.numpy as jnp
import numpy as np
from jax import lax
from jax.experimental import pallas as pl
from jax.experimental.pallas import tpu as pltpu
from jax.sharding import PartitionSpec as P

SWEEPS = 4
SECTIONS = 4
LANES = 128
SUB = 8
PAD = 8
UN = 4
PL = 2

MESH = pl.DeviceIdType.MESH
FOLD = 4.0 ** (1.0 / 3.0)
POWER = -1.0 / (3.0 * float(np.log(2.0)))


def roll(x, shift):
    return pltpu.roll(x, shift, 1)


def kernel(
    n,
    m,
    R,
    L,
    LG,
    segs_out,
    vel_in,
    rate_in,
    warm_in,
    grav,
    slide,
    icy,
    bed,
    vel_out,
    temp_out,
    hard_out,
    U0,
    U1,
    T0,
    T1,
    rate,
    coef,
    temp_st,
    hard_st,
    cb,
    pk,
    crx,
    mg,
    hx,
    tpk,
    trx,
    tmg,
    loc_sem,
    vs_sem,
    vr_sem,
    ts_sem,
    tr_sem,
    ws_sem,
    wr_sem,
    os_sem,
    or_sem,
    hs_sem,
):
    t = lax.axis_index("tile")
    g = lax.axis_index("grp")
    U = (U0, U1)
    T = (T0, T1)
    f32 = jnp.float32
    NS = R // SUB
    TOP = PAD + R
    Q = L // 4
    O, I = 0, 1
    SEGS = {O: ((0, Q), (L - Q, L)), I: ((Q, L - Q),)}

    def th_segs(k, G):
        if G == O:
            return ((0, Q - k), (L - Q + k, L))
        return ((Q - k, L - Q + k),)

    vel_cp = {
        G: [
            pltpu.make_async_copy(
                vel_in.at[:, a:b], U0.at[:, a:b, PAD:TOP, :], loc_sem.at[2 * G + i]
            )
            for i, (a, b) in enumerate(SEGS[G])
        ]
        for G in (O, I)
    }
    rate_cp = pltpu.make_async_copy(rate_in, rate, loc_sem.at[4])
    warm_cp = pltpu.make_async_copy(
        warm_in.at[:, :, pl.ds(pl.multiple_of(g * LANES, LANES), LANES)],
        T0.at[pl.ds(1 + g * LG, LG), PAD:TOP, :],
        loc_sem.at[5],
    )
    for G in (O, I):
        for cp in vel_cp[G]:
            cp.start()
    rate_cp.start()
    warm_cp.start()

    lo_t, hi_t, lo_g, hi_g = t > 0, t < n - 1, g > 0, g < m - 1

    def has(dt, dg):
        ok = None
        for d, lo, hi in ((dt, lo_t, hi_t), (dg, lo_g, hi_g)):
            if d:
                c = lo if d < 0 else hi
                ok = c if ok is None else jnp.logical_and(ok, c)
        return ok

    zero = jnp.zeros((SUB, LANES), f32)

    def clear_rows(l, c):
        for slot in range(2):
            for f in range(2):
                U[slot][f, l, 0:PAD, :] = zero
                U[slot][f, l, TOP : TOP + SUB, :] = zero
            T[slot][l + 1, 0:PAD, :] = zero
            T[slot][l + 1, TOP : TOP + SUB, :] = zero
        return c

    lax.fori_loop(0, L, clear_rows, 0)
    for slot in range(2):
        for l in (0, L + 1):
            T[slot][l] = jnp.zeros_like(T[slot][l])
    crx[...] = jnp.zeros_like(crx)
    trx[...] = jnp.zeros_like(trx)

    barrier = pltpu.get_barrier_semaphore()
    around = [(-1, -1), (-1, 0), (-1, 1), (1, -1), (1, 0), (1, 1)]
    for dt, dg in around:

        @pl.when(has(dt, dg))
        def _(dt=dt, dg=dg):
            pl.semaphore_signal(
                barrier, inc=1, device_id=(t + dt, g + dg), device_id_type=MESH
            )

    for d in range(1, m):
        pl.semaphore_signal(
            barrier, inc=1, device_id=(t, lax.rem(g + d, m)), device_id_type=MESH
        )

    sides_t = lo_t.astype(jnp.int32) + hi_t.astype(jnp.int32)
    sides_g = lo_g.astype(jnp.int32) + hi_g.astype(jnp.int32)
    pl.semaphore_wait(barrier, m - 1 + sides_t * (1 + sides_g))

    def vel_moves(k, G, part):
        slot = k % 2
        moves = []
        if part != "col":
            for a, b in SEGS[G]:
                if k == 0:
                    top, low = vel_in.at[:, a:b, R - 1, :], vel_in.at[:, a:b, 0, :]
                else:
                    top = U[slot].at[:, a:b, TOP - 1, :]
                    low = U[slot].at[:, a:b, PAD, :]
                moves += [
                    ((1, 0), top, U[slot].at[:, a:b, PAD - 1, :]),
                    ((-1, 0), low, U[slot].at[:, a:b, TOP, :]),
                ]
        if part != "row":
            moves += [
                ((0, 1), pk.at[k, G, PAD:TOP], crx.at[k, G, 0, PAD:TOP]),
                ((0, -1), pk.at[k, G, PAD:TOP], crx.at[k, G, 1, PAD:TOP]),
            ]
            if k < SWEEPS:
                for dg, side in ((1, 0), (-1, 1)):
                    moves += [
                        ((1, dg), pk.at[k, G, TOP - 1], crx.at[k, G, side, PAD - 1]),
                        ((-1, dg), pk.at[k, G, PAD], crx.at[k, G, side, TOP]),
                    ]
        first = 4 if part == "col" else 0
        if part == "all":
            rows = 2 * len(SEGS[G])
            index = list(range(rows)) + list(range(4, 4 + len(moves) - rows))
        else:
            index = list(range(first, first + len(moves)))
        return [
            (mv, vs_sem.at[k, G, j], vr_sem.at[k, G, j]) for mv, j in zip(moves, index)
        ]

    def th_moves(k, G):
        slot = k % 2
        moves = []
        for a, b in th_segs(k, G):
            moves += [
                ((1, 0), T[slot].at[1 + a : 1 + b, TOP - 1, :], T[slot].at[1 + a : 1 + b, PAD - 1, :]),
                ((-1, 0), T[slot].at[1 + a : 1 + b, PAD, :], T[slot].at[1 + a : 1 + b, TOP, :]),
            ]
        moves += [
            ((0, 1), tpk.at[k, G], trx.at[k, G, 0]),
            ((0, -1), tpk.at[k, G], trx.at[k, G, 1]),
        ]
        return [(mv, ts_sem.at[k, G, j], tr_sem.at[k, G, j]) for j, mv in enumerate(moves)]

    def remote(mv, s_sem, r_sem, sign=1):
        (dt, dg), src, dst = mv
        return pltpu.make_async_remote_copy(
            src,
            dst,
            s_sem,
            r_sem,
            device_id=(t + sign * dt, g + sign * dg),
            device_id_type=MESH,
        )

    def send(moves):
        for mv, s_sem, r_sem in moves:

            @pl.when(has(*mv[0]))
            def _(mv=mv, s_sem=s_sem, r_sem=r_sem):
                remote(mv, s_sem, r_sem).start()

    def sent(moves):
        for mv, s_sem, r_sem in moves:

            @pl.when(has(*mv[0]))
            def _(mv=mv, s_sem=s_sem, r_sem=r_sem):
                remote(mv, s_sem, r_sem).wait_send()

    def received(moves):
        for mv, s_sem, r_sem in moves:
            dt, dg = mv[0]

            @pl.when(has(-dt, -dg))
            def _(mv=mv, s_sem=s_sem, r_sem=r_sem):
                remote(mv, s_sem, r_sem, -1).wait_recv()

    up_half = 2 * g < m
    pieces = [(i, p) for i in range(m - 1) for p in range(LG // PL)]

    def target(i):
        asc = i + (i >= g).astype(jnp.int32)
        x = m - 1 - i
        desc = x - (x <= g).astype(jnp.int32)
        return jnp.where(up_half, desc, asc)

    def warm_piece(i, p):
        to = target(i)
        return pltpu.make_async_remote_copy(
            warm_in.at[
                p * PL : (p + 1) * PL, :, pl.ds(pl.multiple_of(to * LANES, LANES), LANES)
            ],
            T0.at[pl.ds(1 + g * LG + p * PL, PL), PAD:TOP, :],
            ws_sem.at[i, p],
            wr_sem.at[g, p],
            device_id=(t, to),
            device_id_type=MESH,
        )

    def warm_recv(src, p):
        part = T0.at[1 + src * LG + p * PL : 1 + src * LG + (p + 1) * PL, PAD:TOP, :]
        return pltpu.make_async_remote_copy(
            part, part, ws_sem.at[0, p], wr_sem.at[src, p], device_id=(t, g), device_id_type=MESH
        )

    outer = jnp.logical_or(g * LG < Q, (g + 1) * LG > L - Q)
    SLOTS = 10
    OUTER_SLOTS = {s: (s * 3, s * 3 + 3) for s in range(8)}
    INNER_SLOTS = {4: (0, 4), 5: (4, 8), 6: (8, 12), 7: (12, 18), 8: (18, 24)}

    def bulk(slot):
        for cond, table in ((outer, OUTER_SLOTS), (jnp.logical_not(outer), INNER_SLOTS)):
            if slot in table:
                a, b = table[slot]

                @pl.when(cond)
                def _(a=a, b=b):
                    for i, p in pieces[a:b]:
                        warm_piece(i, p).start()

    def warm_arrived(sources):
        for src in sources:

            @pl.when(g == src)
            def _():
                warm_cp.wait()

            @pl.when(g != src)
            def _(src=src):
                for p in range(LG // PL):
                    warm_recv(src, p).wait_recv()

    lane = lax.broadcasted_iota(jnp.int32, (SUB, LANES), 1)
    first = lane == 0
    last = lane == LANES - 1
    odd = lax.rem(lane, 2) == 1
    pair = lax.div(lane, 2)

    def sides(x, edge):
        up = jnp.where(last, edge, roll(x, LANES - 1))
        down = jnp.where(first, edge, roll(x, 1))
        return up, down

    def rows(s, d=0):
        return slice(PAD + s * SUB + d, PAD + s * SUB + d + SUB)

    def tile(s):
        return slice(s * SUB, (s + 1) * SUB)

    def base(G, a):
        return a if G == O and a < Q else (a - L // 2 if G == O else a - Q)

    def levels(a, b, body):
        steps = -(-(b - a) // UN)

        def step(i, c):
            body(jnp.minimum(a + i * UN, b - UN))
            return c

        lax.fori_loop(0, steps, step, 0)

    def spots(j):
        pu = 2 * j
        return (
            (pair == j, pu + 1, lax.rem(2 * LANES - 2 - pu, LANES)),
            (
                pair == j + LANES // 4,
                lax.rem(pu + LANES // 2 + 1, LANES),
                lax.rem(2 * LANES - 2 - LANES // 2 - pu, LANES),
            ),
        )

    def put_pack(k, G, s, sp, new):
        acc = pk[k, G, rows(s), :]
        for (hit, to, _), x in zip(sp, new):
            acc = jnp.where(hit, roll(x, to), acc)
        pk[k, G, rows(s), :] = acc

    def pack_first(G):
        for a, b in SEGS[G]:
            off = a - base(G, a)

            def body(l0, off=off):
                for j in range(UN):
                    l = l0 + j
                    sp = spots(l - off)
                    for s in range(NS):
                        put_pack(0, G, s, sp, [U0[f, l, rows(s), :] for f in range(2)])

            levels(a, b, body)

    def merge(k, G):
        for s in range(-1, NS + 1):
            w = jnp.where(odd, crx[k, G, 1, rows(s), :], roll(crx[k, G, 0, rows(s), :], 2))
            mg[G, rows(s), :] = w
        if k < SWEEPS:
            for s in range(NS):
                hx[G, tile(s), :] = mg[G, rows(s, 1), :] - mg[G, rows(s, -1), :]

    def strain(slot, G, l, s, sp):
        lm = jnp.maximum(l - 1, 0)
        lp = jnp.minimum(l + 1, L - 1)
        V = U[slot]
        halo = mg[G, rows(s), :]
        c, e, w, up, lo = [], [], [], [], []
        for f in range(2):
            c.append(V[f, l, rows(s), :])
            e.append(V[f, l, rows(s, 1), :])
            w.append(V[f, l, rows(s, -1), :])
            up.append(V[f, lp, rows(s), :])
            lo.append(V[f, lm, rows(s), :])
        nn, ss = zip(*[sides(c[f], roll(halo, sp[f][2])) for f in range(2)])
        xu, xv = e[0] - w[0], e[1] - w[1]
        yv = nn[1] - ss[1]
        shear = (nn[0] - ss[0]) + xv
        du, dv = up[0] - lo[0], up[1] - lo[1]
        total = (xu * (xu + yv) + yv * yv) + 0.25 * (
            (shear * shear + du * du) + dv * dv
        )
        visc = rate[l, tile(s), :] * jnp.exp2(jnp.log(total + 0.04) * POWER)
        return c, e, w, up, lo, nn, ss, xu, xv, total, visc

    def sweep(k, G):
        slot, new_slot = k % 2, (k + 1) % 2
        for a, b in SEGS[G]:
            off = a - base(G, a)

            def body(l0, off=off):
                for j in range(UN):
                    l = l0 + j
                    sp = spots(l - off)
                    for s in range(NS):
                        _, e, w, up, lo, nn, ss, xu, xv, _, visc = strain(slot, G, l, s, sp)
                        hxv = hx[G, tile(s), :]
                        nu, su = sides(xu, roll(hxv, sp[0][2]))
                        nv, sv = sides(xv, roll(hxv, sp[1][2]))
                        near_u = (
                            4.0 * ((e[0] + w[0]) + (up[0] + lo[0]))
                            + (nn[0] + ss[0])
                            + 0.75 * (nv - sv)
                        )
                        near_v = (
                            4.0 * ((nn[1] + ss[1]) + (up[1] + lo[1]))
                            + (e[1] + w[1])
                            + 0.75 * (nu - su)
                        )
                        diagonal = 22.0 * visc + cb[3 + jnp.minimum(l, 1), tile(s), :]
                        scale = cb[0, tile(s), :] / diagonal
                        new = (
                            (cb[1, tile(s), :] + visc * near_u) * scale,
                            (cb[2, tile(s), :] + visc * near_v) * scale,
                        )
                        for f in range(2):
                            U[new_slot][f, l, rows(s), :] = new[f]
                        put_pack(k + 1, G, s, sp, new)

            levels(a, b, body)

    def heat(G):
        slot = SWEEPS % 2
        for a, b in SEGS[G]:
            off = a - base(G, a)

            def body(l0, off=off):
                for j in range(UN):
                    l = l0 + j
                    sp = spots(l - off)
                    for s in range(NS):
                        c, *_, total, visc = strain(slot, G, l, s, sp)
                        q = (cb[0, tile(s), :] * (0.025 * FOLD)) * (visc * total)
                        u, v = 0.05 * c[0], 0.05 * c[1]
                        west = 0.1 + jnp.maximum(u, 0.0)
                        east = 0.1 - jnp.minimum(u, 0.0)
                        south = 0.1 + jnp.maximum(v, 0.0)
                        north = 0.1 - jnp.minimum(v, 0.0)
                        mid = 0.6 - ((west + east) + (south + north))
                        for i, x in enumerate((q, west, east, south, north, mid)):
                            coef[i, l, tile(s), :] = x

            levels(a, b, body)

    def put_tpack(k, G, l, s, x):
        tpk[k, G, tile(s), :] = jnp.where(
            pair == l, roll(x, 2 * l + 1), tpk[k, G, tile(s), :]
        )

    def theta_first(G):
        for a, b in th_segs(0, G):

            def body(l0):
                for j in range(UN):
                    l = l0 + j
                    for s in range(NS):
                        put_tpack(0, G, l, s, T0[l + 1, rows(s), :])

            levels(a, b, body)

    def th_merge(k, G):
        for s in range(NS):
            w = jnp.where(odd, trx[k, G, 1, tile(s), :], roll(trx[k, G, 0, tile(s), :], 2))
            if G == I:
                (a, b), = th_segs(k, I)
                mine = jnp.logical_and(lane > 2 * a, lane <= 2 * b)
                w = jnp.where(mine, w, tmg[k, tile(s), :])
            tmg[k, tile(s), :] = w

    def section(k, G):
        slot, new_slot = k % 2, (k + 1) % 2
        for a, b in th_segs(k + 1, G):

            def body(l0):
                for j in range(UN):
                    l = l0 + j
                    for s in range(NS):
                        V = T[slot]
                        c = V[l + 1, rows(s), :]
                        nn, ss = sides(c, roll(tmg[k, tile(s), :], 2 * LANES - 2 - 2 * l - LANES))
                        q, west, east, south, north, mid = [
                            coef[i, l, tile(s), :] for i in range(6)
                        ]
                        value = (
                            (mid * c + 0.2 * (V[l + 2, rows(s), :] + V[l, rows(s), :]))
                            + (west * V[l + 1, rows(s, -1), :] + east * V[l + 1, rows(s, 1), :])
                            + ((south * ss + north * nn) + q)
                        )
                        if k < SECTIONS - 1:
                            T[new_slot][l + 1, rows(s), :] = value
                            put_tpack(k + 1, G, l, s, value)
                        else:
                            temp_st[l, tile(s), :] = value
                            hard_st[l, tile(s), :] = jnp.exp(-0.6 * value)

            levels(a, b, body)

    def temp_move(i):
        q, a, b = segs_out[i][1:]
        src = temp_st.at[a:b]
        dst = temp_out.at[
            a - q * LG : b - q * LG, :, pl.ds(pl.multiple_of(g * LANES, LANES), LANES)
        ]
        far = pltpu.make_async_remote_copy(
            src, dst, os_sem.at[i], or_sem.at[i, g], device_id=(t, q), device_id_type=MESH
        )
        return far, pltpu.make_async_copy(src, dst, os_sem.at[i])

    def temp_send(i):
        q = segs_out[i][1]

        @pl.when(g != q)
        def _():
            temp_move(i)[0].start()

        @pl.when(g == q)
        def _():
            temp_move(i)[1].start()

    def temp_wait(i):
        q, a, b = segs_out[i][1:]

        @pl.when(g != q)
        def _():
            temp_move(i)[0].wait_send()

        @pl.when(g == q)
        def _():
            temp_move(i)[1].wait()
            for src in range(m):
                if src != q:
                    dst = temp_out.at[
                        a - q * LG : b - q * LG, :, src * LANES : (src + 1) * LANES
                    ]
                    pltpu.make_async_remote_copy(
                        dst, dst, os_sem.at[i], or_sem.at[i, src],
                        device_id=(t, g), device_id_type=MESH,
                    ).wait_recv()

    for G in (O, I):
        send(vel_moves(0, G, "row"))
    bulk(0)
    for G in (O, I):
        for cp in vel_cp[G]:
            cp.wait()
        pack_first(G)
        send(vel_moves(0, G, "col"))
    bulk(1)
    ice = icy[...].astype(f32)
    water = (1.0 - ice) * (1.0 / FOLD)
    cb[0] = ice
    cb[1] = grav[0] * (1.0 / FOLD)
    cb[2] = grav[1] * (1.0 / FOLD)
    cb[3] = water + slide[...] * bed[...].astype(f32) * (1.0 / FOLD)
    cb[4] = water
    rate_cp.wait()

    vel_back = {
        G: [
            pltpu.make_async_copy(
                U[SWEEPS % 2].at[:, a:b, PAD:TOP, :], vel_out.at[:, a:b], hs_sem.at[2 * G + i]
            )
            for i, (a, b) in enumerate(SEGS[G])
        ]
        for G in (O, I)
    }
    for k in range(SWEEPS):
        for G in (O, I):
            received(vel_moves(k, G, "all"))
            if k:
                sent(vel_moves(k - 1, G, "all"))
            merge(k, G)
            sweep(k, G)
            send(vel_moves(k + 1, G, "all"))
            bulk(2 + 2 * k + G)
            if k == SWEEPS - 1:
                for cp in vel_back[G]:
                    cp.start()

    def owners(G):
        return sorted({q for q in range(m) for a, b in th_segs(0, G) if a < (q + 1) * LG and b > q * LG})

    def heat_part(G):
        received(vel_moves(SWEEPS, G, "all"))
        merge(SWEEPS, G)
        heat(G)

    def th_part(k, G):
        received(th_moves(k, G))
        th_merge(k, G)
        if k:
            sent(th_moves(k - 1, G))
        section(k, G)
        if k < SECTIONS - 1:
            send(th_moves(k + 1, G))
        else:
            for i, sg in enumerate(segs_out):
                if sg[0] == G:
                    temp_send(i)
            for cp in hard_back[G]:
                cp.start()

    def th_start(G, known=()):
        warm_arrived([q for q in owners(G) if q not in known])
        theta_first(G)
        send(th_moves(0, G))

    hard_back = {
        G: [
            pltpu.make_async_copy(hard_st.at[a:b], hard_out.at[a:b], hs_sem.at[4 + 2 * G + i])
            for i, (a, b) in enumerate(th_segs(SECTIONS, G))
        ]
        for G in (O, I)
    }
    th_start(O)
    heat_part(O)
    th_part(0, O)
    heat_part(I)
    th_start(I, owners(O))
    th_part(1, O)
    th_part(0, I)
    th_part(2, O)
    th_part(1, I)
    th_part(3, O)
    th_part(2, I)
    th_part(3, I)

    for i in range(len(segs_out)):
        temp_wait(i)
    for i, p in pieces:
        warm_piece(i, p).wait_send()
    for G in (O, I):
        for cp in vel_back[G] + hard_back[G]:
            cp.wait()
        sent(vel_moves(SWEEPS - 1, G, "all"))
        sent(vel_moves(SWEEPS, G, "all"))
        sent(th_moves(SECTIONS - 1, G))


def local(n, m, vel, rate, warm, grav, slide, icy, bed):
    _, L, R, Y = vel.shape
    LG = L // m
    assert Y == LANES and R % SUB == 0 and L % (4 * UN) == 0 and LG % PL == 0
    assert 2 * L == LANES and L // 4 > SECTIONS + UN
    f32 = jnp.float32
    Q = L // 4
    cut = SECTIONS
    parts = [(0, 0, Q - cut), (0, L - Q + cut, L), (1, Q - cut, L - Q + cut)]
    segs_out = []
    for G, a, b in parts:
        while a < b:
            q = a // LG
            e = min(b, (q + 1) * LG)
            segs_out.append((G, q, a, e))
            a = e
    segs_out = tuple(segs_out)
    any_spec = pl.BlockSpec(memory_space=pl.ANY)
    vmem = pl.BlockSpec(memory_space=pltpu.VMEM)
    K = SWEEPS + 1
    H = R + 2 * PAD
    V = pltpu.VMEM
    dma = pltpu.SemaphoreType.DMA
    return pl.pallas_call(
        functools.partial(kernel, n, m, R, L, LG, segs_out),
        out_shape=(
            jax.ShapeDtypeStruct(vel.shape, f32),
            jax.ShapeDtypeStruct(warm.shape, f32),
            jax.ShapeDtypeStruct(rate.shape, f32),
        ),
        in_specs=[any_spec] * 3 + [vmem] * 4,
        out_specs=(any_spec,) * 3,
        scratch_shapes=[
            V((2, L, H, LANES), f32),
            V((2, L, H, LANES), f32),
            V((L + 2, H, LANES), f32),
            V((L + 2, H, LANES), f32),
            V((L, R, LANES), f32),
            V((6, L, R, LANES), f32),
            V((L, R, LANES), f32),
            V((L, R, LANES), f32),
            V((5, R, LANES), f32),
            V((K, 2, H, LANES), f32),
            V((K, 2, 2, H, LANES), f32),
            V((2, H, LANES), f32),
            V((2, R, LANES), f32),
            V((SECTIONS, 2, R, LANES), f32),
            V((SECTIONS, 2, 2, R, LANES), f32),
            V((SECTIONS, R, LANES), f32),
            dma((6,)),
            dma((K, 2, 10)),
            dma((K, 2, 10)),
            dma((SECTIONS, 2, 6)),
            dma((SECTIONS, 2, 6)),
            dma((m - 1, LG // PL)),
            dma((m, LG // PL)),
            dma((len(segs_out),)),
            dma((len(segs_out), m)),
            dma((8,)),
        ],
        compiler_params=pltpu.CompilerParams(
            collective_id=0, has_side_effects=True, vmem_limit_bytes=60 * 1024 * 1024
        ),
        name="ice_step",
    )(vel, rate, warm, grav, slide, icy, bed)


def solution(mesh):
    return jax.shard_map(
        functools.partial(local, mesh.shape["tile"], mesh.shape["grp"]),
        mesh=mesh,
        in_specs=(
            P(None, None, "tile", "grp"),
            P(None, "tile", "grp"),
            P("grp", "tile", None),
            P(None, "tile", "grp"),
            P("tile", "grp"),
            P("tile", "grp"),
            P("tile", "grp"),
        ),
        out_specs=(P(None, None, "tile", "grp"), P("grp", "tile", None), P(None, "tile", "grp")),
        check_vma=False,
    )
```

profile of v0, /device:TPU:0, one launch (start us, length us, event | category | flops | bytes accessed | tf_op | source)
XLA Modules:
  0.0 103.6 jit_solution(16959111714334425795)
XLA Ops:
  0.6 97.7 %ice_step.1 = (f32[2,64,32,128]{3,2,1,0:T(8,128)}, f32[16,32,512]{2,1,0:T(8,128)}, f32[64,32,128]{2,1,0:T(8,128)}) custom-call(f32[2,64,32,128]{3,2,1,0:T(8,128)} %vel_in.1, f32[64,32,128]{2,1,0:T(8,128)} %rate_in.1, f32[16,32,512]{2,1,0:T(8,128)} %warm_in.1, f32[2,32,128]{2,1,0:T(8,128)} %grav.1, f32[32,128]{1,0:T(8,128)} %slide.1, s32[32,128]{1,0:T(8,128)} %icy.1, ...), custom_call_target="tpu_custom_call" | custom-call | tf_op jit(solution)/shard_map/ice_step/pallas_call | solution.py:660
  98.4 0.0 copy-start.1
  98.4 0.0 copy-start
  98.4 3.2 %copy.13 = f32[2,64,32,128]{3,2,1,0:T(8,128)} copy(f32[2,64,32,128]{3,2,1,0:T(8,128)} %get-tuple-element.6) | data formatting | bytes 4194304
  101.6 0.0 copy-done.1
  101.6 1.0 copy.14
  102.6 0.0 copy-done
  102.6 1.0 copy.15
Async XLA Ops:
  98.4 3.2 %copy-start.1 = (f32[16,32,512]{2,1,0:T(8,128)S(1)}, f32[16,32,512]{2,1,0:T(8,128)}, u32[]{:S(2)}) copy-start(f32[16,32,512]{2,1,0:T(8,128)} %get-tuple-element.7) | copy-start | bytes 3145732
  98.4 4.2 %copy-start = (f32[64,32,128]{2,1,0:T(8,128)S(1)}, f32[64,32,128]{2,1,0:T(8,128)}, u32[]{:S(2)}) copy-start(f32[64,32,128]{2,1,0:T(8,128)} %get-tuple-element.8) | copy-start | bytes 3145732
where the time goes:
time: 104 us
  Pallas kernels  97.7 us (94%)
  local copies, waits for them, and re-layouts  5.17 us (5%)
    pallas_call x1, Pallas kernels, local(): pl.pallas_call(functools.partial(kernel, n, m, R, L, LG, segs_out), out_s...  97.7 us
    unnamed x7, local copies, waits for them, and re-layouts  5.17 us

commit v1 on v0

--- a/solution.py
+++ b/solution.py
@@ -2,7 +2,6 @@
 
 import jax
 import jax.numpy as jnp
-import numpy as np
 from jax import lax
 from jax.experimental import pallas as pl
 from jax.experimental.pallas import tpu as pltpu
@@ -13,12 +12,12 @@
 LANES = 128
 SUB = 8
 PAD = 8
-UN = 4
+UB = 2
+UT = 4
 PL = 2
 
 MESH = pl.DeviceIdType.MESH
 FOLD = 4.0 ** (1.0 / 3.0)
-POWER = -1.0 / (3.0 * float(np.log(2.0)))
 
 
 def roll(x, shift):
@@ -51,10 +50,15 @@
     temp_st,
     hard_st,
     cb,
+    dya,
+    dyb,
+    sya,
+    syb,
+    nsa,
+    nsb,
     pk,
     crx,
     mg,
-    hx,
     tpk,
     trx,
     tmg,
@@ -251,17 +255,23 @@
                 p * PL : (p + 1) * PL, :, pl.ds(pl.multiple_of(to * LANES, LANES), LANES)
             ],
             T0.at[pl.ds(1 + g * LG + p * PL, PL), PAD:TOP, :],
-            ws_sem.at[i, p],
-            wr_sem.at[g, p],
+            ws_sem,
+            wr_sem.at[g],
             device_id=(t, to),
             device_id_type=MESH,
         )
 
-    def warm_recv(src, p):
-        part = T0.at[1 + src * LG + p * PL : 1 + src * LG + (p + 1) * PL, PAD:TOP, :]
+    def warm_recv(src):
+        part = T0.at[1 + src * LG : 1 + (src + 1) * LG, PAD:TOP, :]
         return pltpu.make_async_remote_copy(
-            part, part, ws_sem.at[0, p], wr_sem.at[src, p], device_id=(t, g), device_id_type=MESH
+            part, part, ws_sem, wr_sem.at[src], device_id=(t, g), device_id_type=MESH
         )
+
+    def warm_sent():
+        part = temp_st.at[0 : (m - 1) * LG]
+        pltpu.make_async_remote_copy(
+            part, part, ws_sem, wr_sem.at[0], device_id=(t, g), device_id_type=MESH
+        ).wait_send()
 
     outer = jnp.logical_or(g * LG < Q, (g + 1) * LG > L - Q)
     SLOTS = 10
@@ -287,19 +297,14 @@
 
             @pl.when(g != src)
             def _(src=src):
-                for p in range(LG // PL):
-                    warm_recv(src, p).wait_recv()
+                warm_recv(src).wait_recv()
 
     lane = lax.broadcasted_iota(jnp.int32, (SUB, LANES), 1)
     first = lane == 0
     last = lane == LANES - 1
     odd = lax.rem(lane, 2) == 1
     pair = lax.div(lane, 2)
-
-    def sides(x, edge):
-        up = jnp.where(last, edge, roll(x, LANES - 1))
-        down = jnp.where(first, edge, roll(x, 1))
-        return up, down
+    bottom = lax.broadcasted_iota(jnp.int32, (SUB, LANES), 0) == SUB - 1
 
     def rows(s, d=0):
         return slice(PAD + s * SUB + d, PAD + s * SUB + d + SUB)
@@ -307,153 +312,203 @@
     def tile(s):
         return slice(s * SUB, (s + 1) * SUB)
 
-    def base(G, a):
-        return a if G == O and a < Q else (a - L // 2 if G == O else a - Q)
-
-    def levels(a, b, body):
-        steps = -(-(b - a) // UN)
-
-        def step(i, c):
-            body(jnp.minimum(a + i * UN, b - UN))
+    HB = L // 2 // (2 * UB)
+
+    def start_of(G, i):
+        i = jnp.minimum(i, HB - 1) * (2 * UB)
+        if G == I:
+            return i + Q, i
+        return i + jnp.where(i >= Q, L // 2, 0), i
+
+    def edge_spot(j):
+        return (
+            lax.rem(2 * LANES - 2 - 2 * j, LANES),
+            lax.rem(2 * LANES - 2 - LANES // 2 - 2 * j, LANES),
+        )
+
+    def pack_spot(j):
+        return (
+            (pair == j, 2 * j + 1),
+            (pair == j + LANES // 4, lax.rem(2 * j + LANES // 2 + 1, LANES)),
+        )
+
+    def pack_vel(k, G, l, j):
+        for d in range(UB):
+            sp = pack_spot(j + d)
+            for s in range(NS):
+                for f in range(2):
+                    hit, to = sp[f]
+                    pltpu.store(
+                        pk.at[k, G, rows(s), :],
+                        roll(U[k % 2][f, l + d, rows(s), :], to),
+                        mask=hit,
+                    )
+
+    def pack_first(G):
+        def body(i, c):
+            l, j = start_of(G, i)
+            pack_vel(0, G, l, j)
+            pack_vel(0, G, l + UB, j + UB)
             return c
 
-        lax.fori_loop(0, steps, step, 0)
-
-    def spots(j):
-        pu = 2 * j
-        return (
-            (pair == j, pu + 1, lax.rem(2 * LANES - 2 - pu, LANES)),
-            (
-                pair == j + LANES // 4,
-                lax.rem(pu + LANES // 2 + 1, LANES),
-                lax.rem(2 * LANES - 2 - LANES // 2 - pu, LANES),
-            ),
-        )
-
-    def put_pack(k, G, s, sp, new):
-        acc = pk[k, G, rows(s), :]
-        for (hit, to, _), x in zip(sp, new):
-            acc = jnp.where(hit, roll(x, to), acc)
-        pk[k, G, rows(s), :] = acc
-
-    def pack_first(G):
-        for a, b in SEGS[G]:
-            off = a - base(G, a)
-
-            def body(l0, off=off):
-                for j in range(UN):
-                    l = l0 + j
-                    sp = spots(l - off)
-                    for s in range(NS):
-                        put_pack(0, G, s, sp, [U0[f, l, rows(s), :] for f in range(2)])
-
-            levels(a, b, body)
+        lax.fori_loop(0, HB, body, 0)
 
     def merge(k, G):
         for s in range(-1, NS + 1):
             w = jnp.where(odd, crx[k, G, 1, rows(s), :], roll(crx[k, G, 0, rows(s), :], 2))
             mg[G, rows(s), :] = w
-        if k < SWEEPS:
-            for s in range(NS):
-                hx[G, tile(s), :] = mg[G, rows(s, 1), :] - mg[G, rows(s, -1), :]
-
-    def strain(slot, G, l, s, sp):
+            if s == -1:
+                low = w
+        mg[G, rows(NS), :] = jnp.where(bottom, low, w)
+
+    def side_vel(k, G, l, j, dy, sy):
+        V = U[k % 2]
+        tiles = NS + 1 if k < SWEEPS else NS
+        for d in range(UB):
+            sp = edge_spot(j + d)
+            for s in range(tiles):
+                halo = mg[G, rows(s), :]
+                for f in range(2):
+                    x = V[f, l + d, rows(s), :]
+                    if s == NS:
+                        x = jnp.where(bottom, V[f, l + d, rows(-1), :], x)
+                    edge = roll(halo, sp[f])
+                    up = jnp.where(last, edge, roll(x, LANES - 1))
+                    down = jnp.where(first, edge, roll(x, 1))
+                    diff = up - down
+                    dy[f, d, rows(s), :] = diff
+                    if s == NS:
+                        dy[f, d, rows(-1), :] = diff
+                    elif k < SWEEPS:
+                        sy[f, d, tile(s), :] = up + down
+
+    def strain(slot, l, d, s, dy):
+        l = l + d
         lm = jnp.maximum(l - 1, 0)
         lp = jnp.minimum(l + 1, L - 1)
         V = U[slot]
-        halo = mg[G, rows(s), :]
-        c, e, w, up, lo = [], [], [], [], []
+        e, w, up, lo = [], [], [], []
         for f in range(2):
-            c.append(V[f, l, rows(s), :])
             e.append(V[f, l, rows(s, 1), :])
             w.append(V[f, l, rows(s, -1), :])
             up.append(V[f, lp, rows(s), :])
             lo.append(V[f, lm, rows(s), :])
-        nn, ss = zip(*[sides(c[f], roll(halo, sp[f][2])) for f in range(2)])
         xu, xv = e[0] - w[0], e[1] - w[1]
-        yv = nn[1] - ss[1]
-        shear = (nn[0] - ss[0]) + xv
+        yv = dy[1, d, rows(s), :]
+        shear = dy[0, d, rows(s), :] + xv
         du, dv = up[0] - lo[0], up[1] - lo[1]
         total = (xu * (xu + yv) + yv * yv) + 0.25 * (
             (shear * shear + du * du) + dv * dv
         )
-        visc = rate[l, tile(s), :] * jnp.exp2(jnp.log(total + 0.04) * POWER)
-        return c, e, w, up, lo, nn, ss, xu, xv, total, visc
+        visc = rate[l, tile(s), :] * jnp.exp2(lax.log2(total + 0.04) * (-1.0 / 3.0))
+        return e, w, up, lo, total, visc
+
+    def new_vel(k, l, dy, sy):
+        slot, new_slot = k % 2, (k + 1) % 2
+        for d in range(UB):
+            low = jnp.minimum(l + d, 1)
+            for s in range(NS):
+                e, w, up, lo, _, visc = strain(slot, l, d, s, dy)
+                cross_u = dy[1, d, rows(s, 1), :] - dy[1, d, rows(s, -1), :]
+                cross_v = dy[0, d, rows(s, 1), :] - dy[0, d, rows(s, -1), :]
+                near_u = (
+                    4.0 * ((e[0] + w[0]) + (up[0] + lo[0]))
+                    + sy[0, d, tile(s), :]
+                    + 0.75 * cross_u
+                )
+                near_v = (
+                    4.0 * (sy[1, d, tile(s), :] + (up[1] + lo[1]))
+                    + (e[1] + w[1])
+                    + 0.75 * cross_v
+                )
+                scale = 1.0 / (22.0 * visc + cb[2 + low, tile(s), :])
+                U[new_slot][0, l + d, rows(s), :] = (cb[0, tile(s), :] + visc * near_u) * scale
+                U[new_slot][1, l + d, rows(s), :] = (cb[1, tile(s), :] + visc * near_v) * scale
+
+    def new_heat(l, dy):
+        slot = SWEEPS % 2
+        for d in range(UB):
+            for s in range(NS):
+                *_, total, visc = strain(slot, l, d, s, dy)
+                q = (0.025 * FOLD) * (visc * total)
+                u = 0.05 * U[slot][0, l + d, rows(s), :]
+                v = 0.05 * U[slot][1, l + d, rows(s), :]
+                west = 0.1 + jnp.maximum(u, 0.0)
+                east = 0.1 - jnp.minimum(u, 0.0)
+                south = 0.1 + jnp.maximum(v, 0.0)
+                north = 0.1 - jnp.minimum(v, 0.0)
+                mid = 0.6 - ((west + east) + (south + north))
+                for i, x in enumerate((q, west, east, south, north, mid)):
+                    coef[i, l + d, tile(s), :] = x
 
     def sweep(k, G):
-        slot, new_slot = k % 2, (k + 1) % 2
-        for a, b in SEGS[G]:
-            off = a - base(G, a)
-
-            def body(l0, off=off):
-                for j in range(UN):
-                    l = l0 + j
-                    sp = spots(l - off)
-                    for s in range(NS):
-                        _, e, w, up, lo, nn, ss, xu, xv, _, visc = strain(slot, G, l, s, sp)
-                        hxv = hx[G, tile(s), :]
-                        nu, su = sides(xu, roll(hxv, sp[0][2]))
-                        nv, sv = sides(xv, roll(hxv, sp[1][2]))
-                        near_u = (
-                            4.0 * ((e[0] + w[0]) + (up[0] + lo[0]))
-                            + (nn[0] + ss[0])
-                            + 0.75 * (nv - sv)
-                        )
-                        near_v = (
-                            4.0 * ((nn[1] + ss[1]) + (up[1] + lo[1]))
-                            + (e[1] + w[1])
-                            + 0.75 * (nu - su)
-                        )
-                        diagonal = 22.0 * visc + cb[3 + jnp.minimum(l, 1), tile(s), :]
-                        scale = cb[0, tile(s), :] / diagonal
-                        new = (
-                            (cb[1, tile(s), :] + visc * near_u) * scale,
-                            (cb[2, tile(s), :] + visc * near_v) * scale,
-                        )
-                        for f in range(2):
-                            U[new_slot][f, l, rows(s), :] = new[f]
-                        put_pack(k + 1, G, s, sp, new)
-
-            levels(a, b, body)
-
-    def heat(G):
-        slot = SWEEPS % 2
-        for a, b in SEGS[G]:
-            off = a - base(G, a)
-
-            def body(l0, off=off):
-                for j in range(UN):
-                    l = l0 + j
-                    sp = spots(l - off)
-                    for s in range(NS):
-                        c, *_, total, visc = strain(slot, G, l, s, sp)
-                        q = (cb[0, tile(s), :] * (0.025 * FOLD)) * (visc * total)
-                        u, v = 0.05 * c[0], 0.05 * c[1]
-                        west = 0.1 + jnp.maximum(u, 0.0)
-                        east = 0.1 - jnp.minimum(u, 0.0)
-                        south = 0.1 + jnp.maximum(v, 0.0)
-                        north = 0.1 - jnp.minimum(v, 0.0)
-                        mid = 0.6 - ((west + east) + (south + north))
-                        for i, x in enumerate((q, west, east, south, north, mid)):
-                            coef[i, l, tile(s), :] = x
-
-            levels(a, b, body)
-
-    def put_tpack(k, G, l, s, x):
-        tpk[k, G, tile(s), :] = jnp.where(
-            pair == l, roll(x, 2 * l + 1), tpk[k, G, tile(s), :]
-        )
+        def side(l, j, dy, sy):
+            side_vel(k, G, l, j, dy, sy)
+
+        def new(l, dy, sy):
+            if k < SWEEPS:
+                new_vel(k, l, dy, sy)
+            else:
+                new_heat(l, dy)
+
+        def pack(l, j):
+            if k < SWEEPS:
+                pack_vel(k + 1, G, l, j)
+
+        side(*start_of(G, 0), dya, sya)
+
+        def body(i, c):
+            l, j = start_of(G, i)
+            lb, jb = start_of(G, jnp.maximum(i - 1, 0))
+            ln, jn = start_of(G, i + 1)
+            pack(lb + UB, jb + UB)
+            new(l, dya, sya)
+            side(l + UB, j + UB, dyb, syb)
+            pack(l, j)
+            new(l + UB, dyb, syb)
+            side(ln, jn, dya, sya)
+            return c
+
+        lax.fori_loop(0, HB, body, 0)
+        l, j = start_of(G, HB - 1)
+        pack(l + UB, j + UB)
+
+    def pack_th(k, G, l):
+        for d in range(UT):
+            hit = pair == l + d
+            for s in range(NS):
+                pltpu.store(
+                    tpk.at[k, G, tile(s), :],
+                    roll(T[k % 2][l + d + 1, rows(s), :], 2 * (l + d) + 1),
+                    mask=hit,
+                )
+
+    def blocks(segs):
+        counts = [-(-(b - a) // UT) for a, b in segs]
+        total = sum(counts) + sum(counts) % 2
+
+        def start(i):
+            i = jnp.minimum(i, sum(counts) - 1)
+            if len(segs) == 1:
+                (a, b), = segs
+                return jnp.minimum(a + i * UT, b - UT)
+            (a, b), (c, e) = segs
+            return jnp.where(
+                i < counts[0],
+                jnp.minimum(a + i * UT, b - UT),
+                jnp.minimum(c + (i - counts[0]) * UT, e - UT),
+            )
+
+        return total, start
 
     def theta_first(G):
-        for a, b in th_segs(0, G):
-
-            def body(l0):
-                for j in range(UN):
-                    l = l0 + j
-                    for s in range(NS):
-                        put_tpack(0, G, l, s, T0[l + 1, rows(s), :])
-
-            levels(a, b, body)
+        total, start = blocks(th_segs(0, G))
+
+        def body(i, c):
+            pack_th(0, G, start(i))
+            return c
+
+        lax.fori_loop(0, total, body, 0)
 
     def th_merge(k, G):
         for s in range(NS):
@@ -464,33 +519,53 @@
                 w = jnp.where(mine, w, tmg[k, tile(s), :])
             tmg[k, tile(s), :] = w
 
+    def side_th(k, l, ns):
+        for d in range(UT):
+            to = LANES - 2 - 2 * (l + d)
+            for s in range(NS):
+                x = T[k % 2][l + d + 1, rows(s), :]
+                edge = roll(tmg[k, tile(s), :], to)
+                ns[0, d, tile(s), :] = jnp.where(last, edge, roll(x, LANES - 1))
+                ns[1, d, tile(s), :] = jnp.where(first, edge, roll(x, 1))
+
+    def new_th(k, l, ns):
+        V = T[k % 2]
+        for d in range(UT):
+            x = l + d
+            for s in range(NS):
+                q, west, east, south, north, mid = [coef[i, x, tile(s), :] for i in range(6)]
+                value = (
+                    (mid * V[x + 1, rows(s), :] + 0.2 * (V[x + 2, rows(s), :] + V[x, rows(s), :]))
+                    + (west * V[x + 1, rows(s, -1), :] + east * V[x + 1, rows(s, 1), :])
+                    + ((south * ns[1, d, tile(s), :] + north * ns[0, d, tile(s), :]) + q)
+                )
+                if k < SECTIONS - 1:
+                    T[(k + 1) % 2][x + 1, rows(s), :] = value
+                else:
+                    temp_st[x, tile(s), :] = value
+                    hard_st[x, tile(s), :] = jnp.exp(-0.6 * value)
+
     def section(k, G):
-        slot, new_slot = k % 2, (k + 1) % 2
-        for a, b in th_segs(k + 1, G):
-
-            def body(l0):
-                for j in range(UN):
-                    l = l0 + j
-                    for s in range(NS):
-                        V = T[slot]
-                        c = V[l + 1, rows(s), :]
-                        nn, ss = sides(c, roll(tmg[k, tile(s), :], 2 * LANES - 2 - 2 * l - LANES))
-                        q, west, east, south, north, mid = [
-                            coef[i, l, tile(s), :] for i in range(6)
-                        ]
-                        value = (
-                            (mid * c + 0.2 * (V[l + 2, rows(s), :] + V[l, rows(s), :]))
-                            + (west * V[l + 1, rows(s, -1), :] + east * V[l + 1, rows(s, 1), :])
-                            + ((south * ss + north * nn) + q)
-                        )
-                        if k < SECTIONS - 1:
-                            T[new_slot][l + 1, rows(s), :] = value
-                            put_tpack(k + 1, G, l, s, value)
-                        else:
-                            temp_st[l, tile(s), :] = value
-                            hard_st[l, tile(s), :] = jnp.exp(-0.6 * value)
-
-            levels(a, b, body)
+        total, start = blocks(th_segs(k + 1, G))
+
+        def pack(l):
+            if k < SECTIONS - 1:
+                pack_th(k + 1, G, l)
+
+        side_th(k, start(0), nsa)
+
+        def body(i, c):
+            l, lm, ln = start(2 * i), start(2 * i + 1), start(2 * i + 2)
+            pack(start(jnp.maximum(2 * i - 1, 0)))
+            new_th(k, l, nsa)
+            side_th(k, lm, nsb)
+            pack(l)
+            new_th(k, lm, nsb)
+            side_th(k, ln, nsa)
+            return c
+
+        lax.fori_loop(0, total // 2, body, 0)
+        pack(start(total - 1))
 
     def temp_move(i):
         q, a, b = segs_out[i][1:]
@@ -545,12 +620,20 @@
     bulk(1)
     ice = icy[...].astype(f32)
     water = (1.0 - ice) * (1.0 / FOLD)
-    cb[0] = ice
-    cb[1] = grav[0] * (1.0 / FOLD)
-    cb[2] = grav[1] * (1.0 / FOLD)
-    cb[3] = water + slide[...] * bed[...].astype(f32) * (1.0 / FOLD)
-    cb[4] = water
+    cb[0] = ice * grav[0] * (1.0 / FOLD)
+    cb[1] = ice * grav[1] * (1.0 / FOLD)
+    cb[2] = water + slide[...] * bed[...].astype(f32) * (1.0 / FOLD)
+    cb[3] = water
+    cb[4] = ice
     rate_cp.wait()
+
+    def ice_rate(i, c):
+        for d in range(UT):
+            for s in range(NS):
+                rate[i * UT + d, tile(s), :] = rate[i * UT + d, tile(s), :] * cb[4, tile(s), :]
+        return c
+
+    lax.fori_loop(0, L // UT, ice_rate, 0)
 
     vel_back = {
         G: [
@@ -580,7 +663,7 @@
     def heat_part(G):
         received(vel_moves(SWEEPS, G, "all"))
         merge(SWEEPS, G)
-        heat(G)
+        sweep(SWEEPS, G)
 
     def th_part(k, G):
         received(th_moves(k, G))
@@ -624,8 +707,7 @@
 
     for i in range(len(segs_out)):
         temp_wait(i)
-    for i, p in pieces:
-        warm_piece(i, p).wait_send()
+    warm_sent()
     for G in (O, I):
         for cp in vel_back[G] + hard_back[G]:
             cp.wait()
@@ -637,8 +719,8 @@
 def local(n, m, vel, rate, warm, grav, slide, icy, bed):
     _, L, R, Y = vel.shape
     LG = L // m
-    assert Y == LANES and R % SUB == 0 and L % (4 * UN) == 0 and LG % PL == 0
-    assert 2 * L == LANES and L // 4 > SECTIONS + UN
+    assert Y == LANES and R % SUB == 0 and L % (16 * UB) == 0 and LG % PL == 0
+    assert 2 * L == LANES and L // 4 >= SECTIONS + UT
     f32 = jnp.float32
     Q = L // 4
     cut = SECTIONS
@@ -676,10 +758,15 @@
             V((L, R, LANES), f32),
             V((L, R, LANES), f32),
             V((5, R, LANES), f32),
+            V((2, UB, H, LANES), f32),
+            V((2, UB, H, LANES), f32),
+            V((2, UB, R, LANES), f32),
+            V((2, UB, R, LANES), f32),
+            V((2, UT, R, LANES), f32),
+            V((2, UT, R, LANES), f32),
             V((K, 2, H, LANES), f32),
             V((K, 2, 2, H, LANES), f32),
             V((2, H, LANES), f32),
-            V((2, R, LANES), f32),
             V((SECTIONS, 2, R, LANES), f32),
             V((SECTIONS, 2, 2, R, LANES), f32),
             V((SECTIONS, R, LANES), f32),
@@ -688,8 +775,8 @@
             dma((K, 2, 10)),
             dma((SECTIONS, 2, 6)),
             dma((SECTIONS, 2, 6)),
-            dma((m - 1, LG // PL)),
-            dma((m, LG // PL)),
+            dma,
+            dma((m,)),
             dma((len(segs_out),)),
             dma((len(segs_out), m)),
             dma((8,)),

time: 104 us -> 93.9 us (0.903)
  Pallas kernels: 97.7 us -> 87.8 us
    pallas_call x1, Pallas kernels: 97.7 us -> 87.8 us  [local(): pl.pallas_call(functools.partial(kernel, n, m, R, L, LG, segs_out), out_s...]
where the time goes in v1:
time: 93.9 us; the launch traced here: 93.6 us
  Pallas kernels  87.8 us (94%)
  local copies, waits for them, and re-layouts  5.17 us (6%)
    pallas_call x1, Pallas kernels, local(): pl.pallas_call(functools.partial(kernel, n, m, R, L, LG, segs_out), out_s...  87.8 us
    unnamed x7, local copies, waits for them, and re-layouts  5.17 us

profile of v1, /device:TPU:0, one launch (start us, length us, event | category | flops | bytes accessed | tf_op | source)
XLA Modules:
  0.0 93.6 jit_solution(16489773973516030734)
XLA Ops:
  0.6 87.8 %ice_step.1 = (f32[2,64,32,128]{3,2,1,0:T(8,128)}, f32[16,32,512]{2,1,0:T(8,128)}, f32[64,32,128]{2,1,0:T(8,128)}) custom-call(f32[2,64,32,128]{3,2,1,0:T(8,128)} %vel_in.1, f32[64,32,128]{2,1,0:T(8,128)} %rate_in.1, f32[16,32,512]{2,1,0:T(8,128)} %warm_in.1, f32[2,32,128]{2,1,0:T(8,128)} %grav.1, f32[32,128]{1,0:T(8,128)} %slide.1, s32[32,128]{1,0:T(8,128)} %icy.1, ...), custom_call_target="tpu_custom_call" | custom-call | tf_op jit(solution)/shard_map/ice_step/pallas_call | solution.py:742
  88.4 0.0 copy-start.1
  88.4 0.0 copy-start
  88.4 3.2 %copy.13 = f32[2,64,32,128]{3,2,1,0:T(8,128)} copy(f32[2,64,32,128]{3,2,1,0:T(8,128)} %get-tuple-element.6) | data formatting | bytes 4194304
  91.7 0.0 copy-done.1
  91.7 1.0 %copy.14 = f32[16,32,512]{2,1,0:T(8,128)} copy(f32[16,32,512]{2,1,0:T(8,128)S(1)} %copy-done.1) | data formatting | bytes 2097152
  92.6 0.0 copy-done
  92.6 1.0 %copy.15 = f32[64,32,128]{2,1,0:T(8,128)} copy(f32[64,32,128]{2,1,0:T(8,128)S(1)} %copy-done) | data formatting | bytes 2097152
Async XLA Ops:
  88.4 3.2 %copy-start.1 = (f32[16,32,512]{2,1,0:T(8,128)S(1)}, f32[16,32,512]{2,1,0:T(8,128)}, u32[]{:S(2)}) copy-start(f32[16,32,512]{2,1,0:T(8,128)} %get-tuple-element.7) | copy-start | bytes 3145732
  88.4 4.2 %copy-start = (f32[64,32,128]{2,1,0:T(8,128)S(1)}, f32[64,32,128]{2,1,0:T(8,128)}, u32[]{:S(2)}) copy-start(f32[64,32,128]{2,1,0:T(8,128)} %get-tuple-element.8) | copy-start | bytes 3145732

commit v2 on v1

--- a/solution.py
+++ b/solution.py
@@ -15,6 +15,8 @@
 UB = 2
 UT = 4
 PL = 2
+OUT_STEP = 2
+IN_START = 40
 
 MESH = pl.DeviceIdType.MESH
 FOLD = 4.0 ** (1.0 / 3.0)
@@ -240,7 +242,6 @@
                 remote(mv, s_sem, r_sem, -1).wait_recv()
 
     up_half = 2 * g < m
-    pieces = [(i, p) for i in range(m - 1) for p in range(LG // PL)]
 
     def target(i):
         asc = i + (i >= g).astype(jnp.int32)
@@ -251,9 +252,7 @@
     def warm_piece(i, p):
         to = target(i)
         return pltpu.make_async_remote_copy(
-            warm_in.at[
-                p * PL : (p + 1) * PL, :, pl.ds(pl.multiple_of(to * LANES, LANES), LANES)
-            ],
+            warm_in.at[pl.ds(p * PL, PL), :, pl.ds(pl.multiple_of(to * LANES, LANES), LANES)],
             T0.at[pl.ds(1 + g * LG + p * PL, PL), PAD:TOP, :],
             ws_sem,
             wr_sem.at[g],
@@ -274,19 +273,27 @@
         ).wait_send()
 
     outer = jnp.logical_or(g * LG < Q, (g + 1) * LG > L - Q)
-    SLOTS = 10
-    OUTER_SLOTS = {s: (s * 3, s * 3 + 3) for s in range(8)}
-    INNER_SLOTS = {4: (0, 4), 5: (4, 8), 6: (8, 12), 7: (12, 18), 8: (18, 24)}
-
-    def bulk(slot):
-        for cond, table in ((outer, OUTER_SLOTS), (jnp.logical_not(outer), INNER_SLOTS)):
-            if slot in table:
-                a, b = table[slot]
-
-                @pl.when(cond)
-                def _(a=a, b=b):
-                    for i, p in pieces[a:b]:
-                        warm_piece(i, p).start()
+    NP = LG // PL
+    COUNT = (m - 1) * NP
+
+    def feed(c):
+        far = (m - 2) * NP
+
+        @pl.when(jnp.logical_and(outer, jnp.logical_and(lax.rem(c, OUT_STEP) == 0, c < OUT_STEP * COUNT)))
+        def _():
+            q = lax.div(c, OUT_STEP)
+            near = q >= far
+            i = jnp.where(near, m - 2, lax.rem(q, m - 2))
+            warm_piece(i, jnp.where(near, q - far, lax.div(q, m - 2))).start()
+
+        @pl.when(
+            jnp.logical_and(
+                jnp.logical_not(outer), jnp.logical_and(c >= IN_START, c < IN_START + COUNT)
+            )
+        )
+        def _():
+            q = c - IN_START
+            warm_piece(lax.rem(q, m - 1), lax.div(q, m - 1)).start()
 
     def warm_arrived(sources):
         for src in sources:
@@ -461,6 +468,8 @@
             l, j = start_of(G, i)
             lb, jb = start_of(G, jnp.maximum(i - 1, 0))
             ln, jn = start_of(G, i + 1)
+            if k < SWEEPS:
+                feed((2 * k + G) * HB + i)
             pack(lb + UB, jb + UB)
             new(l, dya, sya)
             side(l + UB, j + UB, dyb, syb)
@@ -611,13 +620,11 @@
 
     for G in (O, I):
         send(vel_moves(0, G, "row"))
-    bulk(0)
     for G in (O, I):
         for cp in vel_cp[G]:
             cp.wait()
         pack_first(G)
         send(vel_moves(0, G, "col"))
-    bulk(1)
     ice = icy[...].astype(f32)
     water = (1.0 - ice) * (1.0 / FOLD)
     cb[0] = ice * grav[0] * (1.0 / FOLD)
@@ -644,19 +651,6 @@
         ]
         for G in (O, I)
     }
-    for k in range(SWEEPS):
-        for G in (O, I):
-            received(vel_moves(k, G, "all"))
-            if k:
-                sent(vel_moves(k - 1, G, "all"))
-            merge(k, G)
-            sweep(k, G)
-            send(vel_moves(k + 1, G, "all"))
-            bulk(2 + 2 * k + G)
-            if k == SWEEPS - 1:
-                for cp in vel_back[G]:
-                    cp.start()
-
     def owners(G):
         return sorted({q for q in range(m) for a, b in th_segs(0, G) if a < (q + 1) * LG and b > q * LG})
 
@@ -674,9 +668,6 @@
         if k < SECTIONS - 1:
             send(th_moves(k + 1, G))
         else:
-            for i, sg in enumerate(segs_out):
-                if sg[0] == G:
-                    temp_send(i)
             for cp in hard_back[G]:
                 cp.start()
 
@@ -692,18 +683,39 @@
         ]
         for G in (O, I)
     }
-    th_start(O)
+
+    def temp_out_part(G):
+        for i, sg in enumerate(segs_out):
+            if sg[0] == G:
+                temp_send(i)
+
+    for k in range(SWEEPS):
+        for G in (O, I):
+            received(vel_moves(k, G, "all"))
+            if k:
+                sent(vel_moves(k - 1, G, "all"))
+            merge(k, G)
+            sweep(k, G)
+            send(vel_moves(k + 1, G, "all"))
+            if k == SWEEPS - 1:
+                for cp in vel_back[G]:
+                    cp.start()
+                if G == O:
+                    th_start(O)
+
     heat_part(O)
     th_part(0, O)
+    th_start(I, owners(O))
     heat_part(I)
-    th_start(I, owners(O))
     th_part(1, O)
     th_part(0, I)
     th_part(2, O)
     th_part(1, I)
     th_part(3, O)
     th_part(2, I)
+    temp_out_part(O)
     th_part(3, I)
+    temp_out_part(I)
 
     for i in range(len(segs_out)):
         temp_wait(i)
@@ -719,7 +731,8 @@
 def local(n, m, vel, rate, warm, grav, slide, icy, bed):
     _, L, R, Y = vel.shape
     LG = L // m
-    assert Y == LANES and R % SUB == 0 and L % (16 * UB) == 0 and LG % PL == 0
+    assert Y == LANES and R % SUB == 0 and L % (16 * UB) == 0 and LG % PL == 0 and m > 2
+    assert IN_START + (m - 1) * LG // PL <= SWEEPS * L // (2 * UB)
     assert 2 * L == LANES and L // 4 >= SECTIONS + UT
     f32 = jnp.float32
     Q = L // 4

time: 93.9 us -> 87.3 us (0.930)
  the two profiles are of different devices: /device:TPU:0 before, /device:TPU:11 now
where the time goes in v2:
time: 87.3 us; the launch traced here: 87.1 us
  Pallas kernels  81.2 us (93%)
  local copies, waits for them, and re-layouts  5.17 us (6%)
    pallas_call x1, Pallas kernels, local(): pl.pallas_call(functools.partial(kernel, n, m, R, L, LG, segs_out), out_s...  81.2 us
    unnamed x7, local copies, waits for them, and re-layouts  5.17 us

profile of v2, /device:TPU:11, one launch (start us, length us, event | category | flops | bytes accessed | tf_op | source)
XLA Modules:
  0.0 87.1 jit_solution(10413803755024365241)
XLA Ops:
  0.6 81.2 %ice_step.1 = (f32[2,64,32,128]{3,2,1,0:T(8,128)}, f32[16,32,512]{2,1,0:T(8,128)}, f32[64,32,128]{2,1,0:T(8,128)}) custom-call(f32[2,64,32,128]{3,2,1,0:T(8,128)} %vel_in.1, f32[64,32,128]{2,1,0:T(8,128)} %rate_in.1, f32[16,32,512]{2,1,0:T(8,128)} %warm_in.1, f32[2,32,128]{2,1,0:T(8,128)} %grav.1, f32[32,128]{1,0:T(8,128)} %slide.1, s32[32,128]{1,0:T(8,128)} %icy.1, ...), custom_call_target="tpu_custom_call" | custom-call | tf_op jit(solution)/shard_map/ice_step/pallas_call | solution.py:755
  81.9 0.0 copy-start.1
  81.9 0.0 copy-start
  81.9 3.2 %copy.13 = f32[2,64,32,128]{3,2,1,0:T(8,128)} copy(f32[2,64,32,128]{3,2,1,0:T(8,128)} %get-tuple-element.6) | data formatting | bytes 4194304
  85.1 0.0 copy-done.1
  85.1 1.0 %copy.14 = f32[16,32,512]{2,1,0:T(8,128)} copy(f32[16,32,512]{2,1,0:T(8,128)S(1)} %copy-done.1) | data formatting | bytes 2097152
  86.1 0.0 copy-done
  86.1 1.0 %copy.15 = f32[64,32,128]{2,1,0:T(8,128)} copy(f32[64,32,128]{2,1,0:T(8,128)S(1)} %copy-done) | data formatting | bytes 2097152
Async XLA Ops:
  81.9 3.2 %copy-start.1 = (f32[16,32,512]{2,1,0:T(8,128)S(1)}, f32[16,32,512]{2,1,0:T(8,128)}, u32[]{:S(2)}) copy-start(f32[16,32,512]{2,1,0:T(8,128)} %get-tuple-element.7) | copy-start | bytes 3145732
  81.9 4.2 %copy-start = (f32[64,32,128]{2,1,0:T(8,128)S(1)}, f32[64,32,128]{2,1,0:T(8,128)}, u32[]{:S(2)}) copy-start(f32[64,32,128]{2,1,0:T(8,128)} %get-tuple-element.8) | copy-start | bytes 3145732

commit v3 on v2

--- a/solution.py
+++ b/solution.py
@@ -14,9 +14,8 @@
 PAD = 8
 UB = 2
 UT = 4
-PL = 2
-OUT_STEP = 2
-IN_START = 40
+PL = 1
+PARTS = 2
 
 MESH = pl.DeviceIdType.MESH
 FOLD = 4.0 ** (1.0 / 3.0)
@@ -279,21 +278,32 @@
     def feed(c):
         far = (m - 2) * NP
 
-        @pl.when(jnp.logical_and(outer, jnp.logical_and(lax.rem(c, OUT_STEP) == 0, c < OUT_STEP * COUNT)))
-        def _():
-            q = lax.div(c, OUT_STEP)
+        def issue(cond, order, start, num, den):
+            at = lambda x: lax.div(x * num, den)
+            q = at(c - start)
+            for e in range(-(-num // den)):
+
+                @pl.when(
+                    jnp.logical_and(
+                        jnp.logical_and(cond, c >= start),
+                        jnp.logical_and(q + e < at(c - start + 1), q + e < COUNT),
+                    )
+                )
+                def _(e=e):
+                    warm_piece(*order(q + e)).start()
+
+        def far_first(q):
             near = q >= far
-            i = jnp.where(near, m - 2, lax.rem(q, m - 2))
-            warm_piece(i, jnp.where(near, q - far, lax.div(q, m - 2))).start()
-
-        @pl.when(
-            jnp.logical_and(
-                jnp.logical_not(outer), jnp.logical_and(c >= IN_START, c < IN_START + COUNT)
+            return (
+                jnp.where(near, m - 2, lax.rem(q, m - 2)),
+                jnp.where(near, q - far, lax.div(q, m - 2)),
             )
-        )
-        def _():
-            q = c - IN_START
-            warm_piece(lax.rem(q, m - 1), lax.div(q, m - 1)).start()
+
+        def in_turn(q):
+            return lax.rem(q, m - 1), lax.div(q, m - 1)
+
+        issue(outer, far_first, 0, 1, 1)
+        issue(jnp.logical_not(outer), in_turn, 28, 4, 3)
 
     def warm_arrived(sources):
         for src in sources:
@@ -728,11 +738,46 @@
         sent(th_moves(SECTIONS - 1, G))
 
 
+def hand_over_kernel(a, b, c, x, y, z, va, vb, vc, in_sem, out_sem):
+    parts = []
+    for src, mid, dst in ((a, va, x), (c, vc, z), (b, vb, y)):
+        pieces = src.shape[0] if len(src.shape) == 4 else 1
+        for i in range(pieces):
+            for j in range(PARTS):
+                at = (i,) if len(src.shape) == 4 else ()
+                size = src.shape[len(at)] // PARTS
+                at += (slice(j * size, (j + 1) * size),)
+                parts.append((src.at[at], mid.at[at], dst.at[at]))
+    ins = [pltpu.make_async_copy(s, v, in_sem.at[i]) for i, (s, v, _) in enumerate(parts)]
+    outs = [pltpu.make_async_copy(v, d, out_sem.at[i]) for i, (_, v, d) in enumerate(parts)]
+    for cp in ins:
+        cp.start()
+    for cp, back in zip(ins, outs):
+        cp.wait()
+        back.start()
+    for back in outs:
+        back.wait()
+
+
+def hand_over(arrays):
+    any_spec = pl.BlockSpec(memory_space=pl.ANY)
+    count = PARTS * sum(x.shape[0] if x.ndim == 4 else 1 for x in arrays)
+    return pl.pallas_call(
+        hand_over_kernel,
+        out_shape=tuple(jax.ShapeDtypeStruct(x.shape, x.dtype) for x in arrays),
+        in_specs=[any_spec] * 3,
+        out_specs=(any_spec,) * 3,
+        scratch_shapes=[pltpu.VMEM(x.shape, x.dtype) for x in arrays]
+        + [pltpu.SemaphoreType.DMA((count,))] * 2,
+        compiler_params=pltpu.CompilerParams(vmem_limit_bytes=60 * 1024 * 1024),
+        name="hand_over",
+    )(*arrays)
+
+
 def local(n, m, vel, rate, warm, grav, slide, icy, bed):
     _, L, R, Y = vel.shape
     LG = L // m
     assert Y == LANES and R % SUB == 0 and L % (16 * UB) == 0 and LG % PL == 0 and m > 2
-    assert IN_START + (m - 1) * LG // PL <= SWEEPS * L // (2 * UB)
     assert 2 * L == LANES and L // 4 >= SECTIONS + UT
     f32 = jnp.float32
     Q = L // 4
@@ -752,7 +797,7 @@
     H = R + 2 * PAD
     V = pltpu.VMEM
     dma = pltpu.SemaphoreType.DMA
-    return pl.pallas_call(
+    out = pl.pallas_call(
         functools.partial(kernel, n, m, R, L, LG, segs_out),
         out_shape=(
             jax.ShapeDtypeStruct(vel.shape, f32),
@@ -799,6 +844,7 @@
         ),
         name="ice_step",
     )(vel, rate, warm, grav, slide, icy, bed)
+    return hand_over(out)
 
 
 def solution(mesh):

time: 87.3 us -> 84.7 us (0.970)
  the two profiles are of different devices: /device:TPU:11 before, /device:TPU:20 now
where the time goes in v3:
time: 84.7 us; the launch traced here: 84.4 us
  Pallas kernels  83.8 us (99%)
    pallas_call x1, Pallas kernels, local(): pl.pallas_call(functools.partial(kernel, n, m, R, L, LG, segs_out), out_s...  80.2 us
    pallas_call x1, Pallas kernels, hand_over(): pl.pallas_call(hand_over_kernel, out_shape=tuple((jax.ShapeDtypeStruct(x....  3.58 us

profile of v3, /device:TPU:20, one launch (start us, length us, event | category | flops | bytes accessed | tf_op | source)
XLA Modules:
  0.0 84.4 jit_solution(15137196831954422140)
XLA Ops:
  0.6 80.2 %ice_step.1 = (f32[2,64,32,128]{3,2,1,0:T(8,128)}, f32[16,32,512]{2,1,0:T(8,128)}, f32[64,32,128]{2,1,0:T(8,128)}) custom-call(f32[2,64,32,128]{3,2,1,0:T(8,128)} %vel_in.1, f32[64,32,128]{2,1,0:T(8,128)} %rate_in.1, f32[16,32,512]{2,1,0:T(8,128)} %warm_in.1, f32[2,32,128]{2,1,0:T(8,128)} %grav.1, f32[32,128]{1,0:T(8,128)} %slide.1, s32[32,128]{1,0:T(8,128)} %icy.1, ...), custom_call_target="tpu_custom_call" | custom-call | tf_op jit(solution)/shard_map/ice_step/pallas_call | solution.py:800
  80.8 3.6 %hand_over.1 = (f32[2,64,32,128]{3,2,1,0:T(8,128)}, f32[16,32,512]{2,1,0:T(8,128)}, f32[64,32,128]{2,1,0:T(8,128)}) custom-call(f32[2,64,32,128]{3,2,1,0:T(8,128)} %get-tuple-element.6.a, f32[16,32,512]{2,1,0:T(8,128)} %get-tuple-element.7.b, f32[64,32,128]{2,1,0:T(8,128)} %get-tuple-element.8.c), custom_call_target="tpu_custom_call" | custom-call | tf_op jit(solution)/shard_map/hand_over/pallas_call | solution.py:765
